TPU v7x, 32 devices: a whole 2x2x4 slice. The times are simulated.
32 devices in a mesh: guide: 2 (over core), blk: 16 (over z, y, x).
Axes of the slice: x: 2, y: 2, z: 4, core: 2. Of those that a mesh axis runs over, the one named last changes fastest.
Arguments:
- x_cols: bfloat16 [128, 2048], P(None, 'blk'), may hold values from -3 to 3
- queries: bfloat16 [128, 9216], P('blk'), may hold values from -64 to 64
- new_kv: bfloat16 [128, 576], P('blk'), may hold values from -6 to 6
- cache: bfloat16 [2, 128, 256, 576], P('guide', 'blk'), may hold values from -8 to 8
- lengths: int32 [2, 128], P('guide'), may hold values from 2 to 256, as said below
- perm: int32 [128], replicated, may hold values from 0 to 127, each once
- guide_scale: float32 [128], replicated, may hold values from 1.5 to 7.5
- w_uv: bfloat16 [16, 512, 128], replicated, may hold values from -0.75 to 0.75
- w_out: bfloat16 [2048, 2048], P(None, 'blk'), may hold values from -0.125 to 0.125
- mlp_gain: float32 [2048], replicated, may hold values from 0.5 to 1.5
- w_gate: bfloat16 [2048, 10944], P(None, 'blk'), may hold values from -0.125 to 0.125
- w_up: bfloat16 [2048, 10944], P(None, 'blk'), may hold values from -0.125 to 0.125
- w_down: bfloat16 [10944, 2048], P('blk'), may hold values from -0.0546875 to 0.0546875
- head_gain: float32 [2048], replicated, may hold values from 0.5 to 1.5
- w_head: bfloat16 [2048, 102400], P(None, 'blk'), may hold values from -0.125 to 0.125
Outputs:
- guided: bfloat16 [128, 102400], P('guide', 'blk')
Inputs may be any that keep to these rules, and one draw needn't show every extreme that they name: Positions 0 to lengths[g, r] - 1 of request r's cache in group g are live; each group has a request with 256 live positions. Slot s holds request perm[s]; every request has one slot.
All inputs are finite; a program needn't handle non-finite values.
Results may differ from a plain program's by a relative error of at most 0.018.
Values may be sent and summed in bfloat16 or wider, within the bound.
No kernel may reach another device: no remote copies, remote signals or barrier semaphores. Data moves between devices by JAX's collectives and lax.ppermute only.
A program may use at most 128 MiB of HBM per device.

v0:
```python
import jax
import jax.numpy as jnp
from jax import lax
from jax.sharding import PartitionSpec as P

FF = 10944


def partner(value, axis, apart):
    mask = 2**apart
    pairs = [(source, source ^ mask) for source in range(lax.axis_size(axis))]
    return lax.ppermute(value, axis, pairs)


def rms_round(hidden, gain):
    values = hidden.astype(jnp.float32)
    meansq = jnp.mean(values * values, axis=-1, keepdims=True)
    return (values * lax.rsqrt(meansq + 1e-06) * gain).astype(jnp.bfloat16)


def body(
    x_cols,
    queries,
    new_kv,
    cache,
    lengths,
    perm,
    guide_scale,
    w_uv,
    w_out,
    mlp_gain,
    w_gate,
    w_up,
    w_down,
    head_gain,
    w_head,
):
    guide_index = lax.axis_index("guide")
    blk_index = lax.axis_index("blk")
    slots_dev = queries.shape[0]
    heads_count = w_uv.shape[0]
    latent_size = w_uv.shape[1]
    key_width = new_kv.shape[1]
    score_scale = (w_uv.shape[2] + key_width - latent_size) ** (-0.5)
    slot_ids = blk_index * slots_dev + jnp.arange(slots_dev, dtype=jnp.int32)
    owners = jnp.take(perm, slot_ids)
    live_len = jnp.take(lengths[0], owners)
    query_heads = queries.reshape(slots_dev, heads_count, key_width)
    cached_keys = cache[0]
    scores = (
        jnp.einsum("shk,slk->shl", query_heads, cached_keys, preferred_element_type=jnp.float32)
        * score_scale
    )
    own_score = (
        jnp.einsum("shk,sk->sh", query_heads, new_kv, preferred_element_type=jnp.float32)
        * score_scale
    )
    live_mask = (
        jnp.arange(cached_keys.shape[1], dtype=jnp.int32)[None, None, :] < live_len[:, None, None]
    )
    scores = jnp.where(live_mask, scores, jnp.float32(-1e30))
    peak_score = jnp.maximum(jnp.max(scores, axis=-1), own_score)
    probs = jnp.where(live_mask, jnp.exp(scores - peak_score[..., None]), jnp.float32(0.0))
    own_prob = jnp.exp(own_score - peak_score)
    softmax_total = jnp.sum(probs, axis=-1) + own_prob
    weights = (probs / softmax_total[..., None]).astype(jnp.bfloat16)
    own_weight = (own_prob / softmax_total).astype(jnp.bfloat16)
    latent_out = jnp.einsum(
        "shl,slc->shc", weights, cached_keys[:, :, :latent_size], preferred_element_type=jnp.float32
    )
    latent_out = latent_out + own_weight.astype(jnp.float32)[..., None] * new_kv[
        :, None, :latent_size
    ].astype(jnp.float32)
    value_rows = jnp.einsum(
        "shc,hcd->shd", latent_out.astype(jnp.bfloat16), w_uv, preferred_element_type=jnp.float32
    )
    value_rows = value_rows.astype(jnp.bfloat16).reshape(slots_dev, -1)
    attended = jnp.dot(
        lax.all_gather(value_rows, "blk", axis=0, tiled=True),
        w_out,
        preferred_element_type=jnp.float32,
    )
    residual = (x_cols.astype(jnp.float32) + attended).astype(jnp.bfloat16)
    rows_full = lax.all_gather(residual, "blk", axis=1, tiled=True)
    normed = rms_round(rows_full, mlp_gain)
    unit_count = w_gate.shape[1]
    gate_out = jnp.dot(normed, w_gate, preferred_element_type=jnp.float32)
    up_out = jnp.dot(normed, w_up, preferred_element_type=jnp.float32)
    unit_ids = blk_index * unit_count + jnp.arange(unit_count, dtype=jnp.int32)
    hidden = jnp.where(
        unit_ids[None, :] < FF, jax.nn.silu(gate_out) * up_out, jnp.float32(0.0)
    ).astype(jnp.bfloat16)
    partial_sum = jnp.dot(hidden, w_down, preferred_element_type=jnp.float32)
    summed = lax.psum(partial_sum, "blk")
    after_mlp = (rows_full.astype(jnp.float32) + summed).astype(jnp.bfloat16)
    logits = jnp.dot(rms_round(after_mlp, head_gain), w_head, preferred_element_type=jnp.float32)
    request_count = logits.shape[0]
    half_rows = request_count // 2
    slot_scale = jnp.take(guide_scale, perm)
    request_order = (
        jnp.zeros((request_count,), jnp.int32)
        .at[perm]
        .set(jnp.arange(request_count, dtype=jnp.int32))
    )
    own_order = lax.dynamic_slice_in_dim(request_order, guide_index * half_rows, half_rows)
    other_logits = partner(logits.astype(jnp.bfloat16), "guide", 0).astype(logits.dtype)
    cond_logits = jnp.where(guide_index == 0, logits, other_logits)
    uncond_logits = jnp.where(guide_index == 0, other_logits, logits)
    mixed = (uncond_logits + slot_scale[:, None] * (cond_logits - uncond_logits)).astype(
        jnp.bfloat16
    )
    return jnp.take(mixed, own_order, axis=0)


def solution(mesh):
    return jax.shard_map(
        body,
        mesh=mesh,
        in_specs=(
            P(None, "blk"),
            P("blk", None),
            P("blk", None),
            P("guide", "blk", None, None),
            P("guide", None),
            P(),
            P(),
            P(),
            P(None, "blk"),
            P(),
            P(None, "blk"),
            P(None, "blk"),
            P("blk", None),
            P(),
            P(None, "blk"),
        ),
        out_specs=P("guide", "blk"),
        check_vma=False,
    )
```

profile of v0, /device:TPU:0, one launch (start us, length us, event | category | flops | bytes accessed | tf_op | source)
XLA Modules:
  0.0 257.7 jit_solution(10083849745343940406)
XLA Ops:
  6.5 1.2 reshape.73
  7.8 1.3 gather_fusion.2
  9.1 1.3 gather_fusion.3
  10.5 0.7 slice_convert_fusion
  11.2 0.9 fusion.44
  12.1 2.2 fusion.55
  14.3 0.2 fusion.39
  14.6 2.4 fusion.4
  17.0 0.5 fusion.11
  17.5 45.3 %all_gather.6 = bf16[128,2048]{1,0:T(8,128)(2,1)S(1)} all-gather(bf16[8,2048]{1,0:T(8,128)(2,1)S(1)} %fusion.11), channel_id=1, replica_groups=mesh['guide'=2,'blk'=16] {'blk'}, dimensions={0}, use_global_device_ids=true | all-gather | bytes 557056 | tf_op jit(solution)/shard_map/all_gather | solution.py:79
  62.8 0.3 fusion.10
  63.1 38.5 %all_gather.7 = bf16[128,2048]{1,0:T(8,128)(2,1)S(1)} all-gather(bf16[128,128]{1,0:T(8,128)(2,1)S(1)} %fusion.10), channel_id=1, replica_groups=mesh['guide'=2,'blk'=16] {'blk'}, dimensions={1}, use_global_device_ids=true | all-gather | bytes 557056 | tf_op jit(solution)/shard_map/all_gather | solution.py:84
  101.7 0.2 fusion.15
  101.9 3.5 %fusion.34 = f32[128,684]{0,1:T(8,128)} fusion(bf16[2048,684]{0,1:T(8,128)(2,1)} %param.27, bf16[128,2048]{1,0:T(8,128)(2,1)S(1)} %all_gather.7, f32[2048]{0:T(1024)S(1)} %copy-done.7, f32[128]{0:T(128)S(1)} %add_rsqrt_fusion.1), kind=kOutput, calls=%fused_computation.49 | convolution fusion | flops 359661568 | bytes 3684864 | tf_op jit(solution)/shard_map/dot_general | solution.py:87
  105.4 5.0 %fusion.8 = f32[128,2048]{1,0:T(8,128)} fusion(bf16[684,2048]{1,0:T(8,128)(2,1)S(1)} %copy-done, bf16[2048,684]{0,1:T(8,128)(2,1)} %param.28, f32[128,684]{0,1:T(8,128)} %fusion.34, pred[684]{0:T(1024)(128)(4,1)S(1)} %add_compare_fusion, bf16[128,2048]{1,0:T(8,128)(2,1)S(1)} %all_gather.7, f32[2048]{0:T(1024)S(1)} %copy-done.7, f32[128]{0:T(128)S(1)} %add_rsqrt_fusion.1), kind=kOutput, calls=%fused_computation.21 | convolution fusion | flops 718887424 | bytes 7535788 | tf_op jit(solution)/shard_map/dot_general | solution.py:93
  110.5 109.6 %all-reduce.2.cloned.1.call-done = f32[128,2048]{1,0:T(8,128)} async-done(((f32[128,2048]{1,0:T(8,128)}), f32[128,2048]{1,0:T(8,128)}) %all-reduce.2.cloned.1.call-update) | async-done | bytes 1048592 | tf_op jit(solution)/shard_map/psum | solution.py:94
  220.1 1.4 fusion.12
  221.5 14.7 %fusion.56 = (bf16[128,6400]{1,0:T(8,128)(2,1)}, f32[128,6400]{1,0:T(8,128)}) fusion(bf16[2048,6400]{1,0:T(8,128)(2,1)} %param.31, f32[2048]{0:T(1024)S(1)} %copy-done.5, f32[128]{0:T(128)S(1)} %add_rsqrt_fusion, f32[128,2048]{1,0:T(8,128)} %all-reduce.2.cloned.1.call-done, bf16[128,2048]{1,0:T(8,128)(2,1)S(1)} %all_gather.7), kind=kOutput, calls=%fused_computation.90 | convolution fusion | flops 3358097408 | bytes 32711168 | tf_op jit(solution)/shard_map/dot_general | solution.py:96
  236.2 1.2 scatter_custom_fusion
  237.4 1.2 gather_fusion
  238.8 1.3 collective-permute-done
  240.1 4.3 %fusion.3 = bf16[128,6400]{1,0:T(8,128)(2,1)} fusion(f32[128,6400]{1,0:T(8,128)} %get-tuple-element.13, bf16[128,6400]{1,0:T(8,128)(2,1)} %collective-permute-done, f32[128]{0:T(128)S(1)} %and_select_fusion.2, pred[]{:T(512)S(6)} %eq.4), kind=kLoop, calls=%fused_computation.10 | loop fusion | flops 5734400 | bytes 6554113 | tf_op jit(solution)/shard_map/convert_element_type | solution.py:109
  244.4 4.3 %gather_fusion.1 = bf16[64,6400]{1,0:T(8,128)(2,1)} fusion(bf16[128,6400]{1,0:T(8,128)(2,1)} %fusion.3, s32[1024]{0:T(1024)S(1)} %pad_clamp_fusion), kind=kCustom, calls=%fused_computation.3 | custom fusion | bytes 1638656 | tf_op jit(solution)/shard_map/jit(_take)/gather | solution.py:112
  248.7 2.2 broadcast_select_fusion
  (37 shorter events, 0.4 us)
Async XLA Ops:
  6.5 98.9 %copy-start = (bf16[684,2048]{1,0:T(8,128)(2,1)S(1)}, bf16[684,2048]{1,0:T(8,128)(2,1)}, u32[]{:S(2)}) copy-start(bf16[684,2048]{1,0:T(8,128)(2,1)} %param.29) | copy-start | bytes 8404996
  6.5 213.5 %all-reduce.2.cloned.1.call-start = ((), (), s32[]{:S(2)}) async-start(), calls=%async_computation | async-start | bytes 2097152 | tf_op jit(solution)/shard_map/psum | solution.py:94
  14.6 2.4 copy-start.3
  14.6 48.3 %copy-start.4 = (bf16[2048,128]{1,0:T(8,128)(2,1)S(1)}, bf16[2048,128]{1,0:T(8,128)(2,1)}, u32[]{:S(2)}) copy-start(bf16[2048,128]{1,0:T(8,128)(2,1)} %param.25) | copy-start | bytes 1572868
  14.6 48.3 %copy-start.6 = (bf16[128,128]{1,0:T(8,128)(2,1)S(1)}, bf16[128,128]{1,0:T(8,128)(2,1)}, u32[]{:S(2)}) copy-start(bf16[128,128]{1,0:T(8,128)(2,1)} %param.17) | copy-start | bytes 98308
  17.0 84.9 %copy-start.7 = (f32[2048]{0:T(1024)S(1)}, f32[2048]{0:T(1024)}, u32[]{:S(2)}) copy-start(f32[2048]{0:T(1024)} %param.26) | copy-start | bytes 24580
  105.4 116.1 %copy-start.5 = (f32[2048]{0:T(1024)S(1)}, f32[2048]{0:T(1024)}, u32[]{:S(2)}) copy-start(f32[2048]{0:T(1024)} %param.30) | copy-start | bytes 24580
  221.5 14.7 %copy-start.2 = (s32[128]{0:T(128)S(1)}, s32[128]{0:T(128)}, u32[]{:S(2)}) copy-start(s32[128]{0:T(128)} %param.22) | copy-start | bytes 1540
  221.5 15.9 %copy-start.1 = (f32[128]{0:T(128)S(1)}, f32[128]{0:T(128)}, u32[]{:S(2)}) copy-start(f32[128]{0:T(128)} %param.23) | copy-start | bytes 1540
  236.2 3.8 %collective-permute-start = (bf16[128,6400]{1,0:T(8,128)(2,1)}, bf16[128,6400]{1,0:T(8,128)(2,1)}, u32[]{:S(2)}, u32[]{:S(2)}) collective-permute-start(bf16[128,6400]{1,0:T(8,128)(2,1)} %get-tuple-element.12), channel_id=1, source_target_pairs={{0,16},{16,0},{1,17},{17,1},{2,18},{18,2},{3,19},{19,3},{4,20},{20... | collective-permute-start | bytes 4915208 | tf_op jit(solution)/shard_map/ppermute | solution.py:12
Sparse Core Ops, SparseCore 0:
  110.6 109.4 all-reduce.1
where the time goes:
time: 258 us
  waiting for transfers between devices  111 us (43%)
  blocking collectives  83.9 us (33%)
  matrix products  29.5 us (11%)
  between operations  13.5 us (5%)
  local copies, waits for them, and re-layouts  10.7 us (4%)
  other arithmetic  9.26 us (4%)
    psum x1, waiting for transfers between devices, body(): summed = lax.psum(partial_sum, 'blk')  110 us
    all_gather x1, blocking collectives, body(): lax.all_gather(value_rows, 'blk', axis=0, tiled=True)  45.3 us
    all_gather x1, blocking collectives, body(): rows_full = lax.all_gather(residual, 'blk', axis=1, tiled=True)  38.5 us
    dot_general x1, matrix products, body(): jnp.dot(rms_round(after_mlp, head_gain), w_head, preferred_element_type=j...  14.7 us
  transfers between devices with their start and end apart: 2, of which 2 were waited for; matrix products, arithmetic and copies ran while one was open for 1% of the time, Pallas kernels for 0%

commit v1 on v0

--- a/solution.py
+++ b/solution.py
@@ -4,6 +4,16 @@
 from jax.sharding import PartitionSpec as P
 
 FF = 10944
+
+
+def gather_by_hops(x, mesh_axis, along):
+    size = lax.axis_size(mesh_axis)
+    moving, blocks = (x, [x])
+    for _ in range(size - 1):
+        moving = lax.ppermute(moving, mesh_axis, [(i, (i + 1) % size) for i in range(size)])
+        blocks.insert(0, moving)
+    merged = jnp.concatenate(blocks, axis=along)
+    return jnp.roll(merged, (lax.axis_index(mesh_axis) + 1) * x.shape[along], axis=along)
 
 
 def partner(value, axis, apart):
@@ -81,7 +91,7 @@
         preferred_element_type=jnp.float32,
     )
     residual = (x_cols.astype(jnp.float32) + attended).astype(jnp.bfloat16)
-    rows_full = lax.all_gather(residual, "blk", axis=1, tiled=True)
+    rows_full = gather_by_hops(residual, "blk", 1)
     normed = rms_round(rows_full, mlp_gain)
     unit_count = w_gate.shape[1]
     gate_out = jnp.dot(normed, w_gate, preferred_element_type=jnp.float32)

time: 258 us -> 335 us (1.30)
  waiting for transfers between devices: 111 us -> 222 us
  blocking collectives: 83.9 us -> 45.3 us
    ppermute x0 -> x15, waiting for transfers between devices: none -> 113 us  [gather_by_hops(): lax.ppermute(moving, mesh_axis, [(i, (i + 1) % size) for i in range(size)])]
    all_gather x1 -> x0, blocking collectives: 38.5 us -> none  [body(): rows_full = lax.all_gather(residual, 'blk', axis=1, tiled=True)]
  transfers between devices with their start and end apart: 2 -> 17, of which waited for: 2 -> 17; matrix products, arithmetic and copies ran while one was open for 1% -> 1% of each run, Pallas kernels for 0% -> 0%
where the time goes in v1:
time: 335 us; the launch traced here: 334 us
  waiting for transfers between devices  222 us (66%)
  blocking collectives  45.3 us (14%)
  matrix products  30.9 us (9%)
  between operations  13.7 us (4%)
  local copies, waits for them, and re-layouts  11.6 us (3%)
  other arithmetic  10.3 us (3%)
    ppermute x15, waiting for transfers between devices, gather_by_hops(): lax.ppermute(moving, mesh_axis, [(i, (i + 1) % size) for i in range(size)])  113 us
    psum x1, waiting for transfers between devices, body(): summed = lax.psum(partial_sum, 'blk')  108 us
    all_gather x1, blocking collectives, body(): lax.all_gather(value_rows, 'blk', axis=0, tiled=True)  45.3 us
    dot_general x1, matrix products, body(): jnp.dot(rms_round(after_mlp, head_gain), w_head, preferred_element_type=j...  14.6 us
  transfers between devices with their start and end apart: 17, of which 17 were waited for; matrix products, arithmetic and copies ran while one was open for 1% of the time, Pallas kernels for 0%

profile of v1, /device:TPU:0, one launch (start us, length us, event | category | flops | bytes accessed | tf_op | source)
XLA Modules:
  0.0 334.2 jit_solution(17433428767667814144)
XLA Ops:
  12.7 2.2 fusion.58
  15.2 2.4 fusion.4
  18.1 45.3 %all_gather.3 = bf16[128,2048]{1,0:T(8,128)(2,1)S(1)} all-gather(bf16[8,2048]{1,0:T(8,128)(2,1)S(1)} %fusion.11), channel_id=1, replica_groups=mesh['guide'=2,'blk'=16] {'blk'}, dimensions={0}, use_global_device_ids=true | all-gather | bytes 557056 | tf_op jit(solution)/shard_map/all_gather | solution.py:89
  65.1 7.5 %collective-permute-done = bf16[128,128]{0,1:T(8,128)(2,1)S(1)} collective-permute-done((bf16[128,128]{0,1:T(8,128)(2,1)S(1)}, bf16[128,128]{0,1:T(8,128)(2,1)S(1)}, u32[]{:S(2)}, u32[]{:S(2)}) %collective-permute-start) | collective-permute-done | bytes 32800 | tf_op jit(solution)/shard_map/ppermute | solution.py:13
  72.6 7.5 %collective-permute-done.1 = bf16[128,128]{0,1:T(8,128)(2,1)S(1)} collective-permute-done((bf16[128,128]{0,1:T(8,128)(2,1)S(1)}, bf16[128,128]{0,1:T(8,128)(2,1)S(1)}, u32[]{:S(2)}, u32[]{:S(2)}) %collective-permute-start.1) | collective-permute-done | bytes 32800 | tf_op jit(solution)/shard_map/ppermute | solution.py:13
  80.1 7.5 %collective-permute-done.2 = bf16[128,128]{0,1:T(8,128)(2,1)S(1)} collective-permute-done((bf16[128,128]{0,1:T(8,128)(2,1)S(1)}, bf16[128,128]{0,1:T(8,128)(2,1)S(1)}, u32[]{:S(2)}, u32[]{:S(2)}) %collective-permute-start.2) | collective-permute-done | bytes 32800 | tf_op jit(solution)/shard_map/ppermute | solution.py:13
  87.6 7.5 %collective-permute-done.3 = bf16[128,128]{0,1:T(8,128)(2,1)S(1)} collective-permute-done((bf16[128,128]{0,1:T(8,128)(2,1)S(1)}, bf16[128,128]{0,1:T(8,128)(2,1)S(1)}, u32[]{:S(2)}, u32[]{:S(2)}) %collective-permute-start.3) | collective-permute-done | bytes 32800 | tf_op jit(solution)/shard_map/ppermute | solution.py:13
  95.1 7.8 %collective-permute-done.4 = bf16[128,128]{0,1:T(8,128)(2,1)S(1)} collective-permute-done((bf16[128,128]{0,1:T(8,128)(2,1)S(1)}, bf16[128,128]{0,1:T(8,128)(2,1)S(1)}, u32[]{:S(2)}, u32[]{:S(2)}) %collective-permute-start.4) | collective-permute-done | bytes 32800 | tf_op jit(solution)/shard_map/ppermute | solution.py:13
  102.9 7.5 %collective-permute-done.5 = bf16[128,128]{0,1:T(8,128)(2,1)S(1)} collective-permute-done((bf16[128,128]{0,1:T(8,128)(2,1)S(1)}, bf16[128,128]{0,1:T(8,128)(2,1)S(1)}, u32[]{:S(2)}, u32[]{:S(2)}) %collective-permute-start.5) | collective-permute-done | bytes 32800 | tf_op jit(solution)/shard_map/ppermute | solution.py:13
  110.4 7.5 %collective-permute-done.6 = bf16[128,128]{0,1:T(8,128)(2,1)S(1)} collective-permute-done((bf16[128,128]{0,1:T(8,128)(2,1)S(1)}, bf16[128,128]{0,1:T(8,128)(2,1)S(1)}, u32[]{:S(2)}, u32[]{:S(2)}) %collective-permute-start.6) | collective-permute-done | bytes 32800 | tf_op jit(solution)/shard_map/ppermute | solution.py:13
  117.9 7.5 %collective-permute-done.7 = bf16[128,128]{0,1:T(8,128)(2,1)S(1)} collective-permute-done((bf16[128,128]{0,1:T(8,128)(2,1)S(1)}, bf16[128,128]{0,1:T(8,128)(2,1)S(1)}, u32[]{:S(2)}, u32[]{:S(2)}) %collective-permute-start.7) | collective-permute-done | bytes 32800 | tf_op jit(solution)/shard_map/ppermute | solution.py:13
  125.4 7.5 %collective-permute-done.8 = bf16[128,128]{0,1:T(8,128)(2,1)S(1)} collective-permute-done((bf16[128,128]{0,1:T(8,128)(2,1)S(1)}, bf16[128,128]{0,1:T(8,128)(2,1)S(1)}, u32[]{:S(2)}, u32[]{:S(2)}) %collective-permute-start.8) | collective-permute-done | bytes 32800 | tf_op jit(solution)/shard_map/ppermute | solution.py:13
  132.9 7.5 %collective-permute-done.9 = bf16[128,128]{0,1:T(8,128)(2,1)S(1)} collective-permute-done((bf16[128,128]{0,1:T(8,128)(2,1)S(1)}, bf16[128,128]{0,1:T(8,128)(2,1)S(1)}, u32[]{:S(2)}, u32[]{:S(2)}) %collective-permute-start.9) | collective-permute-done | bytes 32800 | tf_op jit(solution)/shard_map/ppermute | solution.py:13
  140.4 7.6 %collective-permute-done.10 = bf16[128,128]{0,1:T(8,128)(2,1)S(1)} collective-permute-done((bf16[128,128]{0,1:T(8,128)(2,1)S(1)}, bf16[128,128]{0,1:T(8,128)(2,1)S(1)}, u32[]{:S(2)}, u32[]{:S(2)}) %collective-permute-start.10) | collective-permute-done | bytes 32800 | tf_op jit(solution)/shard_map/ppermute | solution.py:13
  148.1 7.5 %collective-permute-done.11 = bf16[128,128]{0,1:T(8,128)(2,1)S(1)} collective-permute-done((bf16[128,128]{0,1:T(8,128)(2,1)S(1)}, bf16[128,128]{0,1:T(8,128)(2,1)S(1)}, u32[]{:S(2)}, u32[]{:S(2)}) %collective-permute-start.11) | collective-permute-done | bytes 32800 | tf_op jit(solution)/shard_map/ppermute | solution.py:13
  155.6 7.5 %collective-permute-done.12 = bf16[128,128]{0,1:T(8,128)(2,1)S(1)} collective-permute-done((bf16[128,128]{0,1:T(8,128)(2,1)S(1)}, bf16[128,128]{0,1:T(8,128)(2,1)S(1)}, u32[]{:S(2)}, u32[]{:S(2)}) %collective-permute-start.12) | collective-permute-done | bytes 32800 | tf_op jit(solution)/shard_map/ppermute | solution.py:13
  163.1 7.5 %collective-permute-done.13 = bf16[128,128]{0,1:T(8,128)(2,1)S(1)} collective-permute-done((bf16[128,128]{0,1:T(8,128)(2,1)S(1)}, bf16[128,128]{0,1:T(8,128)(2,1)S(1)}, u32[]{:S(2)}, u32[]{:S(2)}) %collective-permute-start.13) | collective-permute-done | bytes 32800 | tf_op jit(solution)/shard_map/ppermute | solution.py:13
  170.6 7.5 %collective-permute-done.14 = bf16[128,128]{0,1:T(8,128)(2,1)S(1)} collective-permute-done((bf16[128,128]{0,1:T(8,128)(2,1)S(1)}, bf16[128,128]{0,1:T(8,128)(2,1)S(1)}, u32[]{:S(2)}, u32[]{:S(2)}) %collective-permute-start.14) | collective-permute-done | bytes 32800 | tf_op jit(solution)/shard_map/ppermute | solution.py:13
  179.6 2.8 fusion.38
  182.4 6.2 %fusion.8 = f32[128,2048]{0,1:T(8,128)} fusion(bf16[684,2048]{1,0:T(8,128)(2,1)S(1)} %copy-done, bf16[2048,684]{0,1:T(8,128)(2,1)} %param.28, f32[128,684]{0,1:T(8,128)S(1)} %fusion.38, pred[684]{0:T(1024)(128)(4,1)S(1)} %add_compare_fusion, f32[2048]{0:T(1024)S(1)} %copy-done.7, f32[128]{0:T(128)S(1)} %add_rsqrt_fusion.1, bf16[128,4096]{0,1:T(8,128)(2,1)} %copy-done.3, ...), kind=kOutput, calls=%fused_computation.21 | convolution fusion | flops 718887424 | bytes 7552176 | tf_op jit(solution)/shard_map/dot_general | solution.py:103
  188.6 107.7 %all-reduce.2.cloned.1.call-done = f32[128,2048]{0,1:T(8,128)} async-done(((f32[128,2048]{0,1:T(8,128)}), f32[128,2048]{0,1:T(8,128)}) %all-reduce.2.cloned.1.call-update) | async-done | bytes 1048592 | tf_op jit(solution)/shard_map/psum | solution.py:104
  298.0 14.6 %fusion.59 = (bf16[128,6400]{1,0:T(8,128)(2,1)}, f32[128,6400]{1,0:T(8,128)}) fusion(bf16[2048,6400]{1,0:T(8,128)(2,1)} %param.31, bf16[128,2048]{0,1:T(8,128)(2,1)S(1)} %get-tuple-element.9, f32[2048]{0:T(1024)S(1)} %copy-done.5, f32[128]{0:T(128)S(1)} %add_rsqrt_fusion), kind=kOutput, calls=%fused_computation.124 | convolution fusion | flops 3357310976 | bytes 31662592 | tf_op jit(solution)/shard_map/dot_general | solution.py:106
  316.4 4.4 %fusion.3 = bf16[128,6400]{1,0:T(8,128)(2,1)} fusion(f32[128,6400]{1,0:T(8,128)} %get-tuple-element.15, bf16[128,6400]{1,0:T(8,128)(2,1)} %collective-permute-done.15, f32[128]{0:T(128)S(1)} %and_select_fusion.2, pred[]{:T(512)S(6)} %eq.7), kind=kLoop, calls=%fused_computation.10 | loop fusion | flops 5734400 | bytes 6554113 | tf_op jit(solution)/shard_map/convert_element_type | solution.py:119
  320.8 4.3 %gather_fusion.1 = bf16[64,6400]{1,0:T(8,128)(2,1)} fusion(bf16[128,6400]{1,0:T(8,128)(2,1)} %fusion.3, s32[1024]{0:T(1024)S(1)} %pad_clamp_fusion), kind=kCustom, calls=%fused_computation.3 | custom fusion | bytes 1638656 | tf_op jit(solution)/shard_map/jit(_take)/gather | solution.py:122
  (98 shorter events, 17.5 us)
Async XLA Ops:
  6.5 175.8 %copy-start = (bf16[684,2048]{1,0:T(8,128)(2,1)S(1)}, bf16[684,2048]{1,0:T(8,128)(2,1)}, u32[]{:S(2)}) copy-start(bf16[684,2048]{1,0:T(8,128)(2,1)} %param.29) | copy-start | bytes 8404996
  6.5 289.7 %all-reduce.2.cloned.1.call-start = ((), (), s32[]{:S(2)}) async-start(), calls=%async_computation | async-start | bytes 2097152 | tf_op jit(solution)/shard_map/psum | solution.py:104
  15.2 2.4 copy-start.4
  15.2 48.3 %copy-start.6 = (bf16[128,128]{1,0:T(8,128)(2,1)S(1)}, bf16[128,128]{1,0:T(8,128)(2,1)}, u32[]{:S(2)}) copy-start(bf16[128,128]{1,0:T(8,128)(2,1)} %param.17) | copy-start | bytes 98308
  17.6 161.9 %copy-start.7 = (f32[2048]{0:T(1024)S(1)}, f32[2048]{0:T(1024)}, u32[]{:S(2)}) copy-start(f32[2048]{0:T(1024)} %param.26) | copy-start | bytes 24580
  65.0 7.6 %collective-permute-start = (bf16[128,128]{0,1:T(8,128)(2,1)S(1)}, bf16[128,128]{0,1:T(8,128)(2,1)S(1)}, u32[]{:S(2)}, u32[]{:S(2)}) collective-permute-start(bf16[128,128]{0,1:T(8,128)(2,1)S(1)} %fusion.10), channel_id=1, source_target_pairs={{0,1},{1,2},{2,3},{3,4},{4,5},{5,6},{6,7},{7,8},{8,9},{9,10},{10,1... | collective-permute-start | bytes 98312 | tf_op jit(solution)/shard_map/ppermute | solution.py:13
  72.6 7.5 %collective-permute-start.1 = (bf16[128,128]{0,1:T(8,128)(2,1)S(1)}, bf16[128,128]{0,1:T(8,128)(2,1)S(1)}, u32[]{:S(2)}, u32[]{:S(2)}) collective-permute-start(bf16[128,128]{0,1:T(8,128)(2,1)S(1)} %collective-permute-done), channel_id=1, source_target_pairs={{0,1},{1,2},{2,3},{3,4},{4,5},{5,6},{6,7},{7,8},{8,9},{9,10},{10,1... | collective-permute-start | bytes 98312 | tf_op jit(solution)/shard_map/ppermute | solution.py:13
  80.1 7.5 %collective-permute-start.2 = (bf16[128,128]{0,1:T(8,128)(2,1)S(1)}, bf16[128,128]{0,1:T(8,128)(2,1)S(1)}, u32[]{:S(2)}, u32[]{:S(2)}) collective-permute-start(bf16[128,128]{0,1:T(8,128)(2,1)S(1)} %collective-permute-done.1), channel_id=1, source_target_pairs={{0,1},{1,2},{2,3},{3,4},{4,5},{5,6},{6,7},{7,8},{8,9},{9,10},{10,1... | collective-permute-start | bytes 98312 | tf_op jit(solution)/shard_map/ppermute | solution.py:13
  87.6 7.5 %collective-permute-start.3 = (bf16[128,128]{0,1:T(8,128)(2,1)S(1)}, bf16[128,128]{0,1:T(8,128)(2,1)S(1)}, u32[]{:S(2)}, u32[]{:S(2)}) collective-permute-start(bf16[128,128]{0,1:T(8,128)(2,1)S(1)} %collective-permute-done.2), channel_id=1, source_target_pairs={{0,1},{1,2},{2,3},{3,4},{4,5},{5,6},{6,7},{7,8},{8,9},{9,10},{10,1... | collective-permute-start | bytes 98312 | tf_op jit(solution)/shard_map/ppermute | solution.py:13
  95.1 7.8 %collective-permute-start.4 = (bf16[128,128]{0,1:T(8,128)(2,1)S(1)}, bf16[128,128]{0,1:T(8,128)(2,1)S(1)}, u32[]{:S(2)}, u32[]{:S(2)}) collective-permute-start(bf16[128,128]{0,1:T(8,128)(2,1)S(1)} %collective-permute-done.3), channel_id=1, source_target_pairs={{0,1},{1,2},{2,3},{3,4},{4,5},{5,6},{6,7},{7,8},{8,9},{9,10},{10,1... | collective-permute-start | bytes 98312 | tf_op jit(solution)/shard_map/ppermute | solution.py:13
  102.9 7.5 %collective-permute-start.5 = (bf16[128,128]{0,1:T(8,128)(2,1)S(1)}, bf16[128,128]{0,1:T(8,128)(2,1)S(1)}, u32[]{:S(2)}, u32[]{:S(2)}) collective-permute-start(bf16[128,128]{0,1:T(8,128)(2,1)S(1)} %collective-permute-done.4), channel_id=1, source_target_pairs={{0,1},{1,2},{2,3},{3,4},{4,5},{5,6},{6,7},{7,8},{8,9},{9,10},{10,1... | collective-permute-start | bytes 98312 | tf_op jit(solution)/shard_map/ppermute | solution.py:13
  110.4 7.5 %collective-permute-start.6 = (bf16[128,128]{0,1:T(8,128)(2,1)S(1)}, bf16[128,128]{0,1:T(8,128)(2,1)S(1)}, u32[]{:S(2)}, u32[]{:S(2)}) collective-permute-start(bf16[128,128]{0,1:T(8,128)(2,1)S(1)} %collective-permute-done.5), channel_id=1, source_target_pairs={{0,1},{1,2},{2,3},{3,4},{4,5},{5,6},{6,7},{7,8},{8,9},{9,10},{10,1... | collective-permute-start | bytes 98312 | tf_op jit(solution)/shard_map/ppermute | solution.py:13
  117.9 7.5 %collective-permute-start.7 = (bf16[128,128]{0,1:T(8,128)(2,1)S(1)}, bf16[128,128]{0,1:T(8,128)(2,1)S(1)}, u32[]{:S(2)}, u32[]{:S(2)}) collective-permute-start(bf16[128,128]{0,1:T(8,128)(2,1)S(1)} %collective-permute-done.6), channel_id=1, source_target_pairs={{0,1},{1,2},{2,3},{3,4},{4,5},{5,6},{6,7},{7,8},{8,9},{9,10},{10,1... | collective-permute-start | bytes 98312 | tf_op jit(solution)/shard_map/ppermute | solution.py:13
  125.4 7.5 %collective-permute-start.8 = (bf16[128,128]{0,1:T(8,128)(2,1)S(1)}, bf16[128,128]{0,1:T(8,128)(2,1)S(1)}, u32[]{:S(2)}, u32[]{:S(2)}) collective-permute-start(bf16[128,128]{0,1:T(8,128)(2,1)S(1)} %collective-permute-done.7), channel_id=1, source_target_pairs={{0,1},{1,2},{2,3},{3,4},{4,5},{5,6},{6,7},{7,8},{8,9},{9,10},{10,1... | collective-permute-start | bytes 98312 | tf_op jit(solution)/shard_map/ppermute | solution.py:13
  132.9 7.5 %collective-permute-start.9 = (bf16[128,128]{0,1:T(8,128)(2,1)S(1)}, bf16[128,128]{0,1:T(8,128)(2,1)S(1)}, u32[]{:S(2)}, u32[]{:S(2)}) collective-permute-start(bf16[128,128]{0,1:T(8,128)(2,1)S(1)} %collective-permute-done.8), channel_id=1, source_target_pairs={{0,1},{1,2},{2,3},{3,4},{4,5},{5,6},{6,7},{7,8},{8,9},{9,10},{10,1... | collective-permute-start | bytes 98312 | tf_op jit(solution)/shard_map/ppermute | solution.py:13
  140.4 7.6 %collective-permute-start.10 = (bf16[128,128]{0,1:T(8,128)(2,1)S(1)}, bf16[128,128]{0,1:T(8,128)(2,1)S(1)}, u32[]{:S(2)}, u32[]{:S(2)}) collective-permute-start(bf16[128,128]{0,1:T(8,128)(2,1)S(1)} %collective-permute-done.9), channel_id=1, source_target_pairs={{0,1},{1,2},{2,3},{3,4},{4,5},{5,6},{6,7},{7,8},{8,9},{9,10},{10,1... | collective-permute-start | bytes 98312 | tf_op jit(solution)/shard_map/ppermute | solution.py:13
  148.1 7.5 %collective-permute-start.11 = (bf16[128,128]{0,1:T(8,128)(2,1)S(1)}, bf16[128,128]{0,1:T(8,128)(2,1)S(1)}, u32[]{:S(2)}, u32[]{:S(2)}) collective-permute-start(bf16[128,128]{0,1:T(8,128)(2,1)S(1)} %collective-permute-done.10), channel_id=1, source_target_pairs={{0,1},{1,2},{2,3},{3,4},{4,5},{5,6},{6,7},{7,8},{8,9},{9,10},{10,1... | collective-permute-start | bytes 98312 | tf_op jit(solution)/shard_map/ppermute | solution.py:13
  155.6 7.5 %collective-permute-start.12 = (bf16[128,128]{0,1:T(8,128)(2,1)S(1)}, bf16[128,128]{0,1:T(8,128)(2,1)S(1)}, u32[]{:S(2)}, u32[]{:S(2)}) collective-permute-start(bf16[128,128]{0,1:T(8,128)(2,1)S(1)} %collective-permute-done.11), channel_id=1, source_target_pairs={{0,1},{1,2},{2,3},{3,4},{4,5},{5,6},{6,7},{7,8},{8,9},{9,10},{10,1... | collective-permute-start | bytes 98312 | tf_op jit(solution)/shard_map/ppermute | solution.py:13
  163.1 7.5 %collective-permute-start.13 = (bf16[128,128]{0,1:T(8,128)(2,1)S(1)}, bf16[128,128]{0,1:T(8,128)(2,1)S(1)}, u32[]{:S(2)}, u32[]{:S(2)}) collective-permute-start(bf16[128,128]{0,1:T(8,128)(2,1)S(1)} %collective-permute-done.12), channel_id=1, source_target_pairs={{0,1},{1,2},{2,3},{3,4},{4,5},{5,6},{6,7},{7,8},{8,9},{9,10},{10,1... | collective-permute-start | bytes 98312 | tf_op jit(solution)/shard_map/ppermute | solution.py:13
  170.6 7.5 %collective-permute-start.14 = (bf16[128,128]{0,1:T(8,128)(2,1)S(1)}, bf16[128,128]{0,1:T(8,128)(2,1)S(1)}, u32[]{:S(2)}, u32[]{:S(2)}) collective-permute-start(bf16[128,128]{0,1:T(8,128)(2,1)S(1)} %collective-permute-done.13), channel_id=1, source_target_pairs={{0,1},{1,2},{2,3},{3,4},{4,5},{5,6},{6,7},{7,8},{8,9},{9,10},{10,1... | collective-permute-start | bytes 98312 | tf_op jit(solution)/shard_map/ppermute | solution.py:13
  188.5 109.4 %copy-start.5 = (f32[2048]{0:T(1024)S(1)}, f32[2048]{0:T(1024)}, u32[]{:S(2)}) copy-start(f32[2048]{0:T(1024)} %param.30) | copy-start | bytes 24580
  297.9 15.6 %copy-start.1 = (f32[128]{0:T(128)S(1)}, f32[128]{0:T(128)}, u32[]{:S(2)}) copy-start(f32[128]{0:T(128)} %param.23) | copy-start | bytes 1540
  298.0 17.0 %copy-start.2 = (s32[128]{0:T(128)S(1)}, s32[128]{0:T(128)}, u32[]{:S(2)}) copy-start(s32[128]{0:T(128)} %param.22) | copy-start | bytes 1540
  312.6 3.8 %collective-permute-start.15 = (bf16[128,6400]{1,0:T(8,128)(2,1)}, bf16[128,6400]{1,0:T(8,128)(2,1)}, u32[]{:S(2)}, u32[]{:S(2)}) collective-permute-start(bf16[128,6400]{1,0:T(8,128)(2,1)} %get-tuple-element.14), channel_id=1, source_target_pairs={{0,16},{16,0},{1,17},{17,1},{2,18},{18,2},{3,19},{19,3},{4,20},{20... | collective-permute-start | bytes 4915208 | tf_op jit(solution)/shard_map/ppermute | solution.py:22
  (1 other events, 1.0 us)
Sparse Core Ops, SparseCore 0:
  188.7 107.5 all-reduce.1
